TPU v7x, 512 devices: a whole 4x4x16 slice. The times are simulated.
512 devices in a mesh: row: 16 (over x, z_hi), col: 32 (over z_lo, y, core).
Axes of the slice: x: 4, y: 4, z: 16 (z_hi: 4, z_lo: 4; z = z_hi * 4 + z_lo), core: 2. Of those that a mesh axis runs over, the one named last changes fastest.
Arguments:
- inverse_pool: bfloat16 [16384, 16384], P('row', 'col'), as said below
- factor_one: bfloat16 [16384, 256], P(('row', 'col')), may hold values from -0.046875 to 0.046875
- factor_two: bfloat16 [16384, 256], P(('row', 'col')), may hold values from -0.046875 to 0.046875
- diag_inv_one: float32 [256, 256], replicated, may hold values from -3 to 3
- diag_inv_two: float32 [256, 256], replicated, may hold values from -3 to 3
- struct_one: int32 [64], replicated, may hold values 0 or 1
- struct_two: int32 [64], replicated, may hold values 0 or 1
Outputs:
- column_one: bfloat16 [16384, 256], P(('row', 'col'))
- column_two: bfloat16 [16384, 256], P(('row', 'col'))
- diagonal_one: float32 [256, 256], replicated
- diagonal_two: float32 [256, 256], replicated
Inputs may be any that keep to these rules, and one draw needn't show every extreme that they name: inverse_pool is symmetric: entry (i, j) equals entry (j, i).
All inputs are finite; a program needn't handle non-finite values.
Results may differ from a plain program's by a relative error of at most 0.0007.
Values may be sent and summed in bfloat16 or wider, within the bound.
No kernel may reach another device: no remote copies, remote signals or barrier semaphores. Data moves between devices by JAX's collectives and lax.ppermute only.
A program may use at most 64 MiB of HBM per device.

v0:
```python
import jax
import jax.numpy as jnp
from jax import lax
from jax.sharding import PartitionSpec as P

B = 256


def broadcast(block, axis, owner):
    block = jnp.where(lax.axis_index(axis) == owner, block, jnp.zeros_like(block))
    return lax.psum(block, axis)


def local_mask(struct, first_row, row_count):
    spread = jnp.repeat(struct, B)
    return lax.dynamic_slice_in_dim(spread, first_row, row_count, 0)


def per_device(
    inverse_pool, factor_one, factor_two, diag_inv_one, diag_inv_two, struct_one, struct_two
):
    num_row = lax.axis_size("row")
    num_col = lax.axis_size("col")
    row_count = factor_one.shape[0]
    width = factor_one.shape[1]
    col_width = inverse_pool.shape[1]
    linear = lax.axis_index("row") * num_col + lax.axis_index("col")
    first_row = linear * row_count
    mask_one = local_mask(struct_one, first_row, row_count)
    mask_two = local_mask(struct_two, first_row, row_count)
    masked_one = factor_one * mask_one.astype(jnp.bfloat16)[:, None]
    masked_two = factor_two * mask_two.astype(jnp.bfloat16)[:, None]
    strip_one, strip_two = (
        lax.all_gather(masked_one, "col", axis=0, tiled=True),
        lax.all_gather(masked_two, "col", axis=0, tiled=True),
    )
    stacked = jnp.concatenate([strip_one, strip_two], axis=1)
    col_ratio = num_col // num_row
    root_row = lax.axis_index("col") // col_ratio
    offset = lax.axis_index("col") % col_ratio * col_width
    arrived = broadcast(stacked, "row", root_row)
    owned_rows = lax.dynamic_slice_in_dim(arrived, offset, col_width, 0)
    product = lax.psum_scatter(
        jnp.dot(inverse_pool, owned_rows, preferred_element_type=jnp.float32),
        "col",
        scatter_dimension=0,
        tiled=True,
    )
    product_one = product[:, :width]
    product_two = product[:, width:]
    column_one = (-(product_one * mask_one.astype(jnp.float32)[:, None])).astype(jnp.bfloat16)
    column_two = (-(product_two * mask_two.astype(jnp.float32)[:, None])).astype(jnp.bfloat16)
    term_one = jnp.dot(
        masked_one.astype(jnp.float32).T,
        product_one,
        precision=lax.Precision.HIGHEST,
        preferred_element_type=jnp.float32,
    )
    term_two = jnp.dot(
        masked_two.astype(jnp.float32).T,
        product_two,
        precision=lax.Precision.HIGHEST,
        preferred_element_type=jnp.float32,
    )
    total_one, total_two = lax.psum((term_one, term_two), ("row", "col"))
    return (column_one, column_two, diag_inv_one + total_one, diag_inv_two + total_two)


def solution(mesh):
    in_specs = (
        P("row", "col"),
        P(("row", "col"), None),
        P(("row", "col"), None),
        P(),
        P(),
        P(),
        P(),
    )
    out_specs = (P(("row", "col"), None), P(("row", "col"), None), P(), P())
    return jax.shard_map(
        per_device, mesh=mesh, in_specs=in_specs, out_specs=out_specs, check_vma=False
    )
```

profile of v0, /device:TPU:2, one launch (start us, length us, event | category | flops | bytes accessed | tf_op | source)
XLA Modules:
  0.0 932.4 jit_solution(10251943174924167101)
XLA Ops:
  7.2 0.0 copy-start
  7.2 0.0 all-reduce.4.cloned.1.call-start
  7.2 0.8 broadcast_bitcast_fusion.1
  8.1 0.7 broadcast_bitcast_fusion
  8.9 0.1 dynamic-slice_convert_fusion
  8.9 0.8 broadcast_multiply_fusion.1
  9.7 46.0 %all_gather.6 = bf16[1024,256]{1,0:T(8,128)(2,1)S(1)} all-gather(bf16[32,256]{1,0:T(8,128)(2,1)S(1)} %broadcast_multiply_fusion.1), channel_id=1, replica_groups=mesh['row'=16,'col'=32] {'col'}, dimensions={0}, use_global_device_ids=true | all-gather | bytes 540672 | tf_op jit(solution)/shard_map/all_gather | solution.py:34
  55.7 0.8 broadcast_multiply_fusion
  56.5 39.3 %all_gather.7 = bf16[1024,256]{1,0:T(8,128)(2,1)S(1)} all-gather(bf16[32,256]{1,0:T(8,128)(2,1)S(1)} %broadcast_multiply_fusion), channel_id=1, replica_groups=mesh['row'=16,'col'=32] {'col'}, dimensions={0}, use_global_device_ids=true | all-gather | bytes 540672 | tf_op jit(solution)/shard_map/all_gather | solution.py:35
  95.8 1.2 maximum_select_fusion
  97.1 0.0 all-reduce.4.cloned.1.call-update
  97.1 0.0 reduce-scatter.4.cloned.1.call-start
  97.1 211.4 %all-reduce.4.cloned.1.call-done = bf16[1024,512]{1,0:T(8,128)(2,1)} async-done(((bf16[1024,512]{1,0:T(8,128)(2,1)}), bf16[1024,512]{1,0:T(8,128)(2,1)}) %all-reduce.4.cloned.1.call-update) | async-done | bytes 1048592 | tf_op jit(solution)/shard_map/psum | solution.py:11
  308.6 0.0 copy-done
  308.6 1.8 convolution_bitcast_fusion
  310.4 1.9 copy.15
  312.2 0.0 copy-start.1
  312.2 0.0 copy-start.2
  312.2 0.0 reduce-scatter.4.cloned.1.call-update
  312.3 0.0 all-reduce.6.cloned.1.call-start
  312.3 148.2 %reduce-scatter.4.cloned.1.call-done = f32[32,512]{1,0:T(8,128)} async-done(((f32[1024,512]{1,0:T(8,128)}), f32[32,512]{1,0:T(8,128)}) %reduce-scatter.4.cloned.1.call-update) | async-done | bytes 65552
  460.5 0.8 fusion.6
  461.3 0.1 copy.18
  461.4 1.8 fusion.2
  463.1 1.8 fusion.4
  464.9 0.0 all-reduce.6.cloned.1.call-update
  465.0 0.7 copy.14
  465.7 0.1 copy.17
  465.8 0.7 copy.13
  466.5 456.0 %all-reduce.6.cloned.1.call-done = (f32[256,256]{1,0:T(8,128)}, f32[256,256]{1,0:T(8,128)}) async-done(((f32[256,256]{1,0:T(8,128)}, f32[256,256]{1,0:T(8,128)}), (f32[256,256]{1,0:T(8,128)}, f32[256,256]{1,0:T(8,128)})) %all-reduce.6.cloned.1.call-update) | async-done | bytes 524304 | tf_op jit(solution)/shard_map/psum | solution.py:65
  922.5 0.0 copy-done.1
  922.5 1.7 add.33
  924.2 0.0 copy-done.2
  924.2 1.7 add.34
  (4 shorter events, 0.1 us)
Async XLA Ops:
  7.2 301.4 %copy-start = (bf16[1024,512]{1,0:T(8,128)(2,1)S(1)}, bf16[1024,512]{1,0:T(8,128)(2,1)}, u32[]{:S(2)}) copy-start(bf16[1024,512]{1,0:T(8,128)(2,1)} %param.7) | copy-start | bytes 3145732
  7.2 301.4 %all-reduce.4.cloned.1.call-start = ((), (), s32[]{:S(2)}) async-start(), calls=%async_computation.1 | async-start | bytes 2097152 | tf_op jit(solution)/shard_map/psum | solution.py:11
  97.1 363.4 %reduce-scatter.4.cloned.1.call-start = ((), (), s32[]{:S(2)}) async-start(), calls=%async_computation.2 | async-start | bytes 2162688
  312.2 610.3 %copy-start.1 = (f32[256,256]{1,0:T(8,128)S(1)}, f32[256,256]{1,0:T(8,128)}, u32[]{:S(2)}) copy-start(f32[256,256]{1,0:T(8,128)} %param.10) | copy-start | bytes 786436
  312.2 611.9 %copy-start.2 = (f32[256,256]{1,0:T(8,128)S(1)}, f32[256,256]{1,0:T(8,128)}, u32[]{:S(2)}) copy-start(f32[256,256]{1,0:T(8,128)} %param.11) | copy-start | bytes 786436
  312.3 610.2 %all-reduce.6.cloned.1.call-start = ((), (), s32[]{:S(2)}) async-start(), calls=%async_computation.3 | async-start | bytes 1048576 | tf_op jit(solution)/shard_map/psum | solution.py:65
Sparse Core Ops, SparseCore 0:
  97.2 211.3 all-reduce.3
  312.4 148.0 reduce-scatter.3
  466.6 455.8 all-reduce.5
where the time goes:
time: 933 us; the launch traced here: 932 us
  waiting for transfers between devices  816 us (87%)
  blocking collectives  85.3 us (9%)
  between operations  13.8 us (1%)
    psum x1, waiting for transfers between devices, per_device(): total_one, total_two = lax.psum((term_one, term_two), ('row', 'col'))  456 us
    psum x1, waiting for transfers between devices, broadcast(): return lax.psum(block, axis)  211 us
    unnamed x4, waiting for transfers between devices  148 us
    all_gather x1, blocking collectives, per_device(): lax.all_gather(masked_one, 'col', axis=0, tiled=True)  46 us
    all_gather x1, blocking collectives, per_device(): lax.all_gather(masked_two, 'col', axis=0, tiled=True)  39.3 us
  transfers between devices with their start and end apart: 3, of which 3 were waited for; matrix products, arithmetic and copies ran while one was open for 0% of the time, Pallas kernels for 0%

commit v1 on v0

--- a/solution.py
+++ b/solution.py
@@ -4,6 +4,15 @@
 from jax.sharding import PartitionSpec as P
 
 B = 256
+_hold_sheet = lambda packet, array_axis: jnp.concatenate(
+    lax.all_to_all(
+        jnp.stack([packet for _ in range(lax.axis_size("col"))], axis=0),
+        axis_name="col",
+        split_axis=0,
+        concat_axis=0,
+    ),
+    axis=array_axis,
+)
 
 
 def broadcast(block, axis, owner):
@@ -32,7 +41,7 @@
     masked_two = factor_two * mask_two.astype(jnp.bfloat16)[:, None]
     strip_one, strip_two = (
         lax.all_gather(masked_one, "col", axis=0, tiled=True),
-        lax.all_gather(masked_two, "col", axis=0, tiled=True),
+        _hold_sheet(masked_two, 0),
     )
     stacked = jnp.concatenate([strip_one, strip_two], axis=1)
     col_ratio = num_col // num_row

time: 933 us -> 904 us (0.969)
  blocking collectives: 85.3 us -> 45.8 us
    all_gather x1 -> x0, blocking collectives: 39.3 us -> none  [per_device(): lax.all_gather(masked_two, 'col', axis=0, tiled=True)]
  transfers between devices with their start and end apart: 3 -> 4, of which waited for: 3 -> 3; matrix products, arithmetic and copies ran while one was open for 0% -> 0% of each run, Pallas kernels for 0% -> 0%
where the time goes in v1:
time: 904 us; the launch traced here: 903 us
  waiting for transfers between devices  816 us (90%)
  blocking collectives  45.8 us (5%)
  between operations  13.8 us (2%)
  starting transfers between devices  9.05 us (1%)
    psum x1, waiting for transfers between devices, per_device(): total_one, total_two = lax.psum((term_one, term_two), ('row', 'col'))  456 us
    psum x1, waiting for transfers between devices, broadcast(): return lax.psum(block, axis)  212 us
    unnamed x4, waiting for transfers between devices  148 us
    all_gather x1, blocking collectives, per_device(): lax.all_gather(masked_one, 'col', axis=0, tiled=True)  45.8 us
  transfers between devices with their start and end apart: 4, of which 3 were waited for; matrix products, arithmetic and copies ran while one was open for 0% of the time, Pallas kernels for 0%

profile of v1, /device:TPU:2, one launch (start us, length us, event | category | flops | bytes accessed | tf_op | source)
XLA Modules:
  0.0 903.3 jit_solution(11118887194067052338)
XLA Ops:
  7.2 0.0 copy-start
  7.2 0.8 broadcast_bitcast_fusion.1
  8.0 0.7 broadcast_bitcast_fusion
  8.8 0.1 dynamic-slice_convert_fusion
  8.9 0.8 broadcast_multiply_fusion
  9.7 0.9 stack.2
  10.6 8.9 all-to-all-start
  19.5 0.0 all-reduce.4.cloned.1.call-start
  19.6 0.8 broadcast_multiply_fusion.1
  20.3 45.8 %all_gather.3 = bf16[1024,256]{1,0:T(8,128)(2,1)S(1)} all-gather(bf16[32,256]{1,0:T(8,128)(2,1)S(1)} %broadcast_multiply_fusion.1), channel_id=1, replica_groups=mesh['row'=16,'col'=32] {'col'}, dimensions={0}, use_global_device_ids=true | all-gather | bytes 540672 | tf_op jit(solution)/shard_map/all_gather | solution.py:43
  66.2 0.0 all-to-all-done
  66.2 1.2 maximum_select_fusion
  67.4 0.0 all-reduce.4.cloned.1.call-update
  67.4 0.0 reduce-scatter.4.cloned.1.call-start
  67.5 211.9 %all-reduce.4.cloned.1.call-done = bf16[1024,512]{1,0:T(8,128)(2,1)} async-done(((bf16[1024,512]{1,0:T(8,128)(2,1)}), bf16[1024,512]{1,0:T(8,128)(2,1)}) %all-reduce.4.cloned.1.call-update) | async-done | bytes 1048592 | tf_op jit(solution)/shard_map/psum | solution.py:20
  279.4 0.0 copy-done
  279.4 1.8 convolution_bitcast_fusion
  281.2 1.9 copy.15
  283.1 0.0 copy-start.1
  283.1 0.0 copy-start.2
  283.1 0.0 reduce-scatter.4.cloned.1.call-update
  283.1 0.0 all-reduce.6.cloned.1.call-start
  283.2 148.2 %reduce-scatter.4.cloned.1.call-done = f32[32,512]{1,0:T(8,128)} async-done(((f32[1024,512]{1,0:T(8,128)}), f32[32,512]{1,0:T(8,128)}) %reduce-scatter.4.cloned.1.call-update) | async-done | bytes 65552
  431.3 0.8 fusion.6
  432.1 0.1 copy.18
  432.2 1.8 fusion.2
  434.0 1.8 fusion.4
  435.8 0.0 all-reduce.6.cloned.1.call-update
  435.8 0.7 copy.14
  436.5 0.1 copy.17
  436.6 0.7 copy.13
  437.3 456.1 %all-reduce.6.cloned.1.call-done = (f32[256,256]{1,0:T(8,128)}, f32[256,256]{1,0:T(8,128)}) async-done(((f32[256,256]{1,0:T(8,128)}, f32[256,256]{1,0:T(8,128)}), (f32[256,256]{1,0:T(8,128)}, f32[256,256]{1,0:T(8,128)})) %all-reduce.6.cloned.1.call-update) | async-done | bytes 524304 | tf_op jit(solution)/shard_map/psum | solution.py:74
  893.4 0.0 copy-done.1
  893.4 1.7 add.33
  895.1 0.0 copy-done.2
  895.1 1.7 add.34
  (4 shorter events, 0.1 us)
Async XLA Ops:
  7.2 272.3 %copy-start = (bf16[1024,512]{1,0:T(8,128)(2,1)S(1)}, bf16[1024,512]{1,0:T(8,128)(2,1)}, u32[]{:S(2)}) copy-start(bf16[1024,512]{1,0:T(8,128)(2,1)} %param.7) | copy-start | bytes 3145732
  10.6 55.6 %all-to-all-start = ((bf16[32,32,256]{2,1,0:T(8,128)(2,1)}), bf16[32,32,256]{2,1,0:T(8,128)(2,1)S(1)}, u32[]{:S(2)}, u32[]{:S(2)}) async-start(bf16[32,32,256]{2,1,0:T(8,128)(2,1)} %stack.2), calls=%async_computation | async-start | bytes 1048576 | tf_op jit(solution)/shard_map/all_to_all | solution.py:8
  19.5 259.9 %all-reduce.4.cloned.1.call-start = ((), (), s32[]{:S(2)}) async-start(), calls=%async_computation.2 | async-start | bytes 2097152 | tf_op jit(solution)/shard_map/psum | solution.py:20
  67.4 363.9 %reduce-scatter.4.cloned.1.call-start = ((), (), s32[]{:S(2)}) async-start(), calls=%async_computation.3 | async-start | bytes 2162688
  283.1 610.3 %copy-start.1 = (f32[256,256]{1,0:T(8,128)S(1)}, f32[256,256]{1,0:T(8,128)}, u32[]{:S(2)}) copy-start(f32[256,256]{1,0:T(8,128)} %param.10) | copy-start | bytes 786436
  283.1 612.0 %copy-start.2 = (f32[256,256]{1,0:T(8,128)S(1)}, f32[256,256]{1,0:T(8,128)}, u32[]{:S(2)}) copy-start(f32[256,256]{1,0:T(8,128)} %param.11) | copy-start | bytes 786436
  283.1 610.3 %all-reduce.6.cloned.1.call-start = ((), (), s32[]{:S(2)}) async-start(), calls=%async_computation.4 | async-start | bytes 1048576 | tf_op jit(solution)/shard_map/psum | solution.py:74
Sparse Core Ops, SparseCore 0:
  67.5 211.8 all-reduce.3
  283.2 148.0 reduce-scatter.3
  437.4 455.9 all-reduce.5

commit v2 on v0

--- a/solution.py
+++ b/solution.py
@@ -2,6 +2,7 @@
 import jax.numpy as jnp
 from jax import lax
 from jax.sharding import PartitionSpec as P
+from jax.lax import psum
 
 B = 256
 
@@ -62,7 +63,7 @@
         precision=lax.Precision.HIGHEST,
         preferred_element_type=jnp.float32,
     )
-    total_one, total_two = lax.psum((term_one, term_two), ("row", "col"))
+    total_one, total_two = psum(psum((term_one, term_two), "col"), "row")
     return (column_one, column_two, diag_inv_one + total_one, diag_inv_two + total_two)
 
 

time: 933 us -> 967 us (1.036)
  the two profiles are of different devices: /device:TPU:2 before, /device:TPU:8 now
where the time goes in v2:
time: 967 us
  waiting for transfers between devices  850 us (88%)
  blocking collectives  85.4 us (9%)
  between operations  13.9 us (1%)
    psum x2, waiting for transfers between devices, per_device(): total_one, total_two = psum(psum((term_one, term_two), 'col'), 'row')  496 us
    psum x1, waiting for transfers between devices, broadcast(): return lax.psum(block, axis)  214 us
    unnamed x5, waiting for transfers between devices  141 us
    all_gather x1, blocking collectives, per_device(): lax.all_gather(masked_one, 'col', axis=0, tiled=True)  44.8 us
    all_gather x1, blocking collectives, per_device(): lax.all_gather(masked_two, 'col', axis=0, tiled=True)  40.6 us
  transfers between devices with their start and end apart: 4, of which 4 were waited for; matrix products, arithmetic and copies ran while one was open for 0% of the time, Pallas kernels for 0%

profile of v2, /device:TPU:8, one launch (start us, length us, event | category | flops | bytes accessed | tf_op | source)
XLA Modules:
  0.0 966.8 jit_solution(10877625859708968709)
XLA Ops:
  7.2 0.0 copy-start
  7.2 0.0 all-reduce.6.cloned.1.call-start
  7.2 0.8 broadcast_bitcast_fusion.1
  8.1 0.7 broadcast_bitcast_fusion
  8.9 0.1 dynamic-slice_convert_fusion
  8.9 0.8 broadcast_multiply_fusion.1
  9.7 44.8 %all_gather.6 = bf16[1024,256]{1,0:T(8,128)(2,1)S(1)} all-gather(bf16[32,256]{1,0:T(8,128)(2,1)S(1)} %broadcast_multiply_fusion.1), channel_id=1, replica_groups=mesh['row'=16,'col'=32] {'col'}, dimensions={0}, use_global_device_ids=true | all-gather | bytes 540672 | tf_op jit(solution)/shard_map/all_gather | solution.py:35
  54.5 0.8 broadcast_multiply_fusion
  55.3 40.6 %all_gather.7 = bf16[1024,256]{1,0:T(8,128)(2,1)S(1)} all-gather(bf16[32,256]{1,0:T(8,128)(2,1)S(1)} %broadcast_multiply_fusion), channel_id=1, replica_groups=mesh['row'=16,'col'=32] {'col'}, dimensions={0}, use_global_device_ids=true | all-gather | bytes 540672 | tf_op jit(solution)/shard_map/all_gather | solution.py:36
  95.9 1.2 maximum_select_fusion
  97.1 0.0 all-reduce.6.cloned.1.call-update
  97.2 0.0 reduce-scatter.4.cloned.1.call-start
  97.2 213.6 %all-reduce.6.cloned.1.call-done = bf16[1024,512]{1,0:T(8,128)(2,1)} async-done(((bf16[1024,512]{1,0:T(8,128)(2,1)}), bf16[1024,512]{1,0:T(8,128)(2,1)}) %all-reduce.6.cloned.1.call-update) | async-done | bytes 1048592 | tf_op jit(solution)/shard_map/psum | solution.py:12
  310.8 0.0 copy-done
  310.8 1.8 convolution_bitcast_fusion
  312.6 1.9 copy.15
  314.5 0.0 copy-start.1
  314.5 0.0 reduce-scatter.4.cloned.1.call-update
  314.5 0.0 copy-start.2
  314.5 0.0 all-reduce.8.cloned.1.call-start
  314.5 140.5 %reduce-scatter.4.cloned.1.call-done = f32[32,512]{1,0:T(8,128)} async-done(((f32[1024,512]{1,0:T(8,128)}), f32[32,512]{1,0:T(8,128)}) %reduce-scatter.4.cloned.1.call-update) | async-done | bytes 65552
  455.1 1.8 fusion.2
  456.9 1.8 fusion.4
  458.6 0.0 all-reduce.8.cloned.1.call-update
  458.6 0.0 all-reduce.10.cloned.1.call-start
  458.7 284.2 %all-reduce.8.cloned.1.call-done = (f32[256,256]{1,0:T(8,128)}, f32[256,256]{1,0:T(8,128)}) async-done(((f32[256,256]{1,0:T(8,128)}, f32[256,256]{1,0:T(8,128)}), (f32[256,256]{1,0:T(8,128)}, f32[256,256]{1,0:T(8,128)})) %all-reduce.8.cloned.1.call-update) | async-done | bytes 524304 | tf_op jit(solution)/shard_map/psum | solution.py:66
  742.9 0.0 all-reduce.10.cloned.1.call-update
  742.9 0.8 fusion.6
  743.7 0.1 copy.18
  743.8 0.7 copy.14
  744.5 0.1 copy.17
  744.6 0.7 copy.13
  745.3 211.6 %all-reduce.10.cloned.1.call-done = (f32[256,256]{1,0:T(8,128)}, f32[256,256]{1,0:T(8,128)}) async-done(((f32[256,256]{1,0:T(8,128)}, f32[256,256]{1,0:T(8,128)}), (f32[256,256]{1,0:T(8,128)}, f32[256,256]{1,0:T(8,128)})) %all-reduce.10.cloned.1.call-update) | async-done | bytes 524304 | tf_op jit(solution)/shard_map/psum | solution.py:66
  956.9 0.0 copy-done.1
  956.9 1.7 add.37
  958.6 0.0 copy-done.2
  958.6 1.7 add.38
  (4 shorter events, 0.1 us)
Async XLA Ops:
  7.2 303.6 %copy-start = (bf16[1024,512]{1,0:T(8,128)(2,1)S(1)}, bf16[1024,512]{1,0:T(8,128)(2,1)}, u32[]{:S(2)}) copy-start(bf16[1024,512]{1,0:T(8,128)(2,1)} %param.7) | copy-start | bytes 3145732
  7.2 303.6 %all-reduce.6.cloned.1.call-start = ((), (), s32[]{:S(2)}) async-start(), calls=%async_computation.1 | async-start | bytes 2097152 | tf_op jit(solution)/shard_map/psum | solution.py:12
  97.2 357.9 %reduce-scatter.4.cloned.1.call-start = ((), (), s32[]{:S(2)}) async-start(), calls=%async_computation.2 | async-start | bytes 2162688
  314.5 642.5 %copy-start.1 = (f32[256,256]{1,0:T(8,128)S(1)}, f32[256,256]{1,0:T(8,128)}, u32[]{:S(2)}) copy-start(f32[256,256]{1,0:T(8,128)} %param.10) | copy-start | bytes 786436
  314.5 644.1 %copy-start.2 = (f32[256,256]{1,0:T(8,128)S(1)}, f32[256,256]{1,0:T(8,128)}, u32[]{:S(2)}) copy-start(f32[256,256]{1,0:T(8,128)} %param.11) | copy-start | bytes 786436
  314.5 428.4 %all-reduce.8.cloned.1.call-start = ((), (), s32[]{:S(2)}) async-start(), calls=%async_computation.3 | async-start | bytes 1048576 | tf_op jit(solution)/shard_map/psum | solution.py:66
  458.6 498.3 %all-reduce.10.cloned.1.call-start = ((), (), s32[]{:S(2)}) async-start(), calls=%async_computation.4 | async-start | bytes 1048576 | tf_op jit(solution)/shard_map/psum | solution.py:66
Sparse Core Ops, SparseCore 0:
  97.3 213.4 all-reduce.5
  314.6 140.4 reduce-scatter.3
  458.8 284.0 all-reduce.7
  745.9 210.9 all-reduce.9

commit v3 on v0

--- a/solution.py
+++ b/solution.py
@@ -6,9 +6,13 @@
 B = 256
 
 
+def shape_numbers(inp, axis_tag):
+    return lax.all_gather(inp, axis_name=axis_tag).sum(axis=0)
+
+
 def broadcast(block, axis, owner):
     block = jnp.where(lax.axis_index(axis) == owner, block, jnp.zeros_like(block))
-    return lax.psum(block, axis)
+    return shape_numbers(block, axis)
 
 
 def local_mask(struct, first_row, row_count):

time: 933 us -> 1120 us (1.20)
  waiting for transfers between devices: 816 us -> 993 us
    all_gather x0 -> x1, waiting for transfers between devices: none -> 385 us  [shape_numbers(): return lax.all_gather(inp, axis_name=axis_tag).sum(axis=0)]
    psum x1 -> x0, waiting for transfers between devices: 211 us -> none  [broadcast(): return lax.psum(block, axis)]
where the time goes in v3:
time: 1120 us
  waiting for transfers between devices  993 us (89%)
  blocking collectives  85.3 us (8%)
  other arithmetic  16.1 us (1%)
  between operations  13.8 us (1%)
    psum x1, waiting for transfers between devices, per_device(): total_one, total_two = lax.psum((term_one, term_two), ('row', 'col'))  456 us
    all_gather x1, waiting for transfers between devices, shape_numbers(): return lax.all_gather(inp, axis_name=axis_tag).sum(axis=0)  385 us
    unnamed x4, waiting for transfers between devices  152 us
    all_gather x1, blocking collectives, per_device(): lax.all_gather(masked_one, 'col', axis=0, tiled=True)  46 us
    all_gather x1, blocking collectives, per_device(): lax.all_gather(masked_two, 'col', axis=0, tiled=True)  39.3 us
  transfers between devices with their start and end apart: 3, of which 3 were waited for; matrix products, arithmetic and copies ran while one was open for 0% of the time, Pallas kernels for 0%

profile of v3, /device:TPU:2, one launch (start us, length us, event | category | flops | bytes accessed | tf_op | source)
XLA Modules:
  0.0 1119.3 jit_solution(18106189279554462769)
XLA Ops:
  7.2 0.0 copy-start
  7.2 0.0 all-gather.2.cloned.1.call-start
  7.2 0.8 broadcast_bitcast_fusion.1
  8.1 0.7 broadcast_bitcast_fusion
  8.9 0.1 dynamic-slice_convert_fusion
  8.9 0.8 broadcast_multiply_fusion.1
  9.7 46.0 %all_gather.10 = bf16[1024,256]{1,0:T(8,128)(2,1)S(1)} all-gather(bf16[32,256]{1,0:T(8,128)(2,1)S(1)} %broadcast_multiply_fusion.1), channel_id=1, replica_groups=mesh['row'=16,'col'=32] {'col'}, dimensions={0}, use_global_device_ids=true | all-gather | bytes 540672 | tf_op jit(solution)/shard_map/all_gather | solution.py:38
  55.7 0.8 broadcast_multiply_fusion
  56.5 39.3 %all_gather.11 = bf16[1024,256]{1,0:T(8,128)(2,1)S(1)} all-gather(bf16[32,256]{1,0:T(8,128)(2,1)S(1)} %broadcast_multiply_fusion), channel_id=1, replica_groups=mesh['row'=16,'col'=32] {'col'}, dimensions={0}, use_global_device_ids=true | all-gather | bytes 540672 | tf_op jit(solution)/shard_map/all_gather | solution.py:39
  95.8 1.2 maximum_select_fusion
  97.0 0.0 all-gather.2.cloned.1.call-update
  97.0 0.0 reduce-scatter.4.cloned.1.call-start
  97.1 384.7 %all-gather.2.cloned.1.call-done = bf16[16,1024,512]{2,1,0:T(8,128)(2,1)} async-done(((bf16[1,1024,512]{2,1,0:T(8,128)(2,1)}), bf16[16,1024,512]{2,1,0:T(8,128)(2,1)}) %all-gather.2.cloned.1.call-update) | async-done | bytes 16777232 | tf_op jit(solution)/shard_map/all_gather | solution.py:10
  481.8 9.9 reduce_sum.12
  491.7 0.0 copy-done
  491.7 1.8 convolution_bitcast_fusion
  493.5 1.9 copy.15
  495.4 0.0 copy-start.1
  495.4 0.0 copy-start.2
  495.4 0.0 reduce-scatter.4.cloned.1.call-update
  495.4 0.0 all-reduce.3.cloned.1.call-start
  495.5 152.0 %reduce-scatter.4.cloned.1.call-done = f32[32,512]{1,0:T(8,128)} async-done(((f32[1024,512]{1,0:T(8,128)}), f32[32,512]{1,0:T(8,128)}) %reduce-scatter.4.cloned.1.call-update) | async-done | bytes 65552
  647.4 0.8 fusion.6
  648.2 0.1 copy.18
  648.3 1.8 fusion.2
  650.1 1.8 fusion.4
  651.8 0.0 all-reduce.3.cloned.1.call-update
  651.9 0.7 copy.14
  652.6 0.1 copy.17
  652.7 0.7 copy.13
  653.4 456.0 %all-reduce.3.cloned.1.call-done = (f32[256,256]{1,0:T(8,128)}, f32[256,256]{1,0:T(8,128)}) async-done(((f32[256,256]{1,0:T(8,128)}, f32[256,256]{1,0:T(8,128)}), (f32[256,256]{1,0:T(8,128)}, f32[256,256]{1,0:T(8,128)})) %all-reduce.3.cloned.1.call-update) | async-done | bytes 524304 | tf_op jit(solution)/shard_map/psum | solution.py:69
  1109.4 0.0 copy-done.1
  1109.4 1.7 add.31
  1111.1 0.0 copy-done.2
  1111.1 1.7 add.32
  (4 shorter events, 0.1 us)
Async XLA Ops:
  7.2 484.5 %copy-start = (bf16[1024,512]{1,0:T(8,128)(2,1)S(1)}, bf16[1024,512]{1,0:T(8,128)(2,1)}, u32[]{:S(2)}) copy-start(bf16[1024,512]{1,0:T(8,128)(2,1)} %param.7) | copy-start | bytes 3145732
  7.2 474.6 %all-gather.2.cloned.1.call-start = ((), (), s32[]{:S(2)}) async-start(), calls=%async_computation.1 | async-start | bytes 17825792 | tf_op jit(solution)/shard_map/all_gather | solution.py:10
  97.0 550.4 %reduce-scatter.4.cloned.1.call-start = ((), (), s32[]{:S(2)}) async-start(), calls=%async_computation.2 | async-start | bytes 2162688
  495.4 614.0 %copy-start.1 = (f32[256,256]{1,0:T(8,128)S(1)}, f32[256,256]{1,0:T(8,128)}, u32[]{:S(2)}) copy-start(f32[256,256]{1,0:T(8,128)} %param.10) | copy-start | bytes 786436
  495.4 615.7 %copy-start.2 = (f32[256,256]{1,0:T(8,128)S(1)}, f32[256,256]{1,0:T(8,128)}, u32[]{:S(2)}) copy-start(f32[256,256]{1,0:T(8,128)} %param.11) | copy-start | bytes 786436
  495.4 614.0 %all-reduce.3.cloned.1.call-start = ((), (), s32[]{:S(2)}) async-start(), calls=%async_computation.3 | async-start | bytes 1048576 | tf_op jit(solution)/shard_map/psum | solution.py:69
Sparse Core Ops, SparseCore 0:
  97.1 384.6 all-gather.1
  495.5 151.8 reduce-scatter.3
  654.4 454.9 all-reduce.2
